TPU v7x, 512 devices: a whole 4x8x8 slice. The times are simulated.
512 devices in a mesh: phi: 8 (over z), theta: 16 (over y, core), row: 4 (over x).
Axes of the slice: x: 4, y: 8, z: 8, core: 2. Of those that a mesh axis runs over, the one named last changes fastest.
Arguments:
- fields: float32 [8, 12, 1536, 2048], P(None, 'row', 'phi', 'theta'), may hold values from -6 to 6
- kept_counts: int32 [512], replicated, may hold values from 1 to 384, as said below
Outputs:
- filtered: float32 [8, 12, 1536, 2048], P(None, 'row', 'phi', 'theta')
Inputs may be any that keep to these rules, and one draw needn't show every extreme that they name: `kept_counts`: modes 0 to count - 1 of a cap row are kept; some row reaches 384 in every draw.
All inputs are finite; a program needn't handle non-finite values.
Results may differ from a plain program's by a relative error of at most 0.00007.
Values sent between devices are 32-bit elements; how exact they have to be, the bound alone decides.
No kernel may reach another device: no remote copies, remote signals or barrier semaphores. Data moves between devices by JAX's collectives and lax.ppermute only.
A program may use at most 64 MiB of HBM per device.

v0:
```python
import math

import jax
import jax.numpy as jnp
from jax import lax
from jax.sharding import PartitionSpec as P

KMAX = 384


def tables(offset, span_rows, points, mode_count):
    azimuth = offset + jnp.arange(span_rows, dtype=jnp.int32)
    wavenumber = jnp.arange(mode_count, dtype=jnp.int32)
    phase_turns = azimuth[:, None] * wavenumber[None, :] % points
    angles = phase_turns.astype(jnp.float32) * (2.0 * math.pi / points)
    forward = jnp.concatenate([jnp.cos(angles), jnp.sin(angles)], axis=1)
    weight = jnp.where(wavenumber == 0, 1.0, 2.0).astype(jnp.float32) / points
    weight = jnp.concatenate([weight, weight])
    backward = (forward * weight[None, :]).T
    return (forward, backward)


def spectral(lines, row_counts):
    nfields, shells, local_points, rows_here = lines.shape
    n_phi = lax.axis_size("phi")
    points = local_points * n_phi
    highest = lax.Precision.HIGHEST
    groups = nfields * shells
    grouped = lines.reshape(groups, local_points, rows_here)
    line_counts = jnp.broadcast_to(row_counts[None, :], (groups, rows_here)).reshape(-1)
    phi_index = lax.axis_index("phi")
    forward, backward = tables(phi_index * local_points, local_points, points, KMAX)
    share_rows = forward.shape[1] // n_phi
    out = jnp.einsum(
        "pk,gpr->kgr", forward, grouped, precision=highest, preferred_element_type=jnp.float32
    )
    share = lax.psum_scatter(
        out.reshape(share_rows * lax.axis_size("phi"), groups * rows_here),
        "phi",
        scatter_dimension=0,
        tiled=True,
    )
    share_index = phi_index * share_rows + jnp.arange(share_rows, dtype=jnp.int32)
    keep = (share_index % KMAX)[:, None] < line_counts[None, :]
    masked = jnp.where(keep, share, 0.0)
    piece = lax.all_gather(masked, "phi", axis=0, tiled=True)
    stacked = piece.reshape(piece.shape[0], groups, rows_here)
    result = jnp.einsum(
        "kp,kgr->gpr", backward, stacked, precision=highest, preferred_element_type=jnp.float32
    )
    return result.reshape(lines.shape)


def on_device(fields, kept_counts):
    n_theta = lax.axis_size("theta")
    theta_index = lax.axis_index("theta")
    band_rows = fields.shape[3]
    caps = kept_counts.shape[0] // band_rows
    cap_bands = caps // 2
    count_table = kept_counts.reshape(caps, band_rows)
    piece_rows = band_rows // n_theta
    received = lax.all_to_all(fields, "theta", split_axis=3, concat_axis=3, tiled=True)
    north_end = cap_bands * piece_rows
    south_start = (n_theta - cap_bands) * piece_rows
    cap_lines = jnp.concatenate(
        [received[:, :, :, :north_end], received[:, :, :, south_start:]], axis=3
    )
    row_counts = lax.dynamic_slice_in_dim(
        count_table, theta_index * piece_rows, piece_rows, 1
    ).reshape(-1)
    smoothed = spectral(cap_lines, row_counts)
    rebuilt = jnp.concatenate(
        [
            smoothed[:, :, :, :north_end],
            received[:, :, :, north_end:south_start],
            smoothed[:, :, :, north_end:],
        ],
        axis=3,
    )
    return lax.all_to_all(rebuilt, "theta", split_axis=3, concat_axis=3, tiled=True)


def solution(mesh):
    placed = (P(None, "row", "phi", "theta"), P())
    return jax.shard_map(
        on_device,
        mesh=mesh,
        in_specs=placed,
        out_specs=P(None, "row", "phi", "theta"),
        check_vma=False,
    )
```

profile of v0, /device:TPU:1, one launch (start us, length us, event | category | flops | bytes accessed | tf_op | source)
XLA Modules:
  0.0 286.2 jit_solution(12094316669807166460)
XLA Ops:
  6.5 0.0 copy-start
  6.5 3.6 %copy.26 = f32[8,3,192,128]{2,0,1,3:T(8,128)} copy(f32[8,3,192,128]{3,2,1,0:T(8,128)} %param.2) | data formatting | bytes 4718592 | tf_op args[0]
  10.1 10.4 %all-to-all-start = ((f32[8,3,192,128]{2,0,1,3:T(8,128)}), f32[8,3,192,128]{2,0,1,3:T(8,128)S(1)}, u32[]{:S(2)}, u32[]{:S(2)}) async-start(f32[8,3,192,128]{2,0,1,3:T(8,128)} %copy.26), calls=%async_computation | async-start | bytes 6291456 | tf_op jit(solution)/shard_map/all_to_all | solution.py:62
  20.5 0.0 reduce-scatter.2.cloned.1.call-start
  20.5 2.1 fusion.10
  22.6 68.9 %all-to-all-done = f32[8,3,192,128]{2,0,1,3:T(8,128)S(1)} async-done(((f32[8,3,192,128]{2,0,1,3:T(8,128)}), f32[8,3,192,128]{2,0,1,3:T(8,128)S(1)}, u32[]{:S(2)}, u32[]{:S(2)}) %all-to-all-start) | async-done | bytes 2359328 | tf_op jit(solution)/shard_map/all_to_all | solution.py:62
  91.5 0.1 fusion.14
  91.5 0.1 copy.27
  91.7 0.1 copy.28
  91.8 0.1 pad_maximum_fusion.1
  91.9 0.7 copy-done.2
  92.6 5.4 %fusion.3 = f32[768,768]{1,0:T(8,128)} fusion(f32[768,192]{1,0:T(8,128)S(1)} %bitcast.17, f32[192,384]{1,0:T(8,128)S(1)} %copy-done.2, f32[192,384]{1,0:T(8,128)S(1)} %get-tuple-element.9), kind=kOutput, calls=%fused_computation.6 | convolution fusion | flops 1359101952 | bytes 3538944 | tf_op jit(solution)/shard_map/pk,gpr->kgr/dot_general | solution.py:34
  98.0 0.0 reduce-scatter.2.cloned.1.call-update
  98.0 0.0 all-gather.2.cloned.1.call-start
  98.1 0.0 copy-done
  98.1 0.1 constant_dynamic-slice_fusion
  98.1 0.1 broadcast_in_dim.23
  98.2 0.1 lt.33
  98.3 42.2 %reduce-scatter.2.cloned.1.call-done = f32[96,768]{1,0:T(8,128)} async-done(((f32[768,768]{1,0:T(8,128)}), f32[96,768]{1,0:T(8,128)}) %reduce-scatter.2.cloned.1.call-update) | async-done | bytes 294928 | tf_op jit(solution)/shard_map/reduce_scatter | solution.py:37
  140.5 1.8 compare_select_fusion
  142.2 0.0 all-gather.2.cloned.1.call-update
  142.3 44.4 %all-gather.2.cloned.1.call-done = f32[768,768]{1,0:T(8,128)} async-done(((f32[96,768]{1,0:T(8,128)}), f32[768,768]{1,0:T(8,128)}) %all-gather.2.cloned.1.call-update) | async-done | bytes 2359312 | tf_op jit(solution)/shard_map/all_gather | solution.py:46
  186.7 2.0 copy.29
  188.8 2.0 fusion
  190.8 0.0 slice-start
  190.8 0.1 fusion.15
  190.9 0.2 copy.33
  191.1 0.2 copy.34
  191.4 1.1 slice-done
  192.5 0.2 pad_maximum_fusion
  192.7 84.5 %all_to_all.10 = f32[8,3,192,128]{2,0,1,3:T(8,128)S(1)} all-to-all(f32[8,3,192,128]{2,0,1,3:T(8,128)S(1)} %pad_maximum_fusion), channel_id=1, replica_groups=mesh['phi'=8,'theta'=16,'row'=4] {'theta'}, dimensions={3} | all-to-all | bytes 4718592 | tf_op jit(solution)/shard_map/all_to_all | solution.py:80
  277.2 2.1 copy.32
  (10 shorter events, 0.0 us)
Async XLA Ops:
  6.5 91.5 %copy-start = (s32[512]{0:T(512)S(1)}, s32[512]{0:T(512)}, u32[]{:S(2)}) copy-start(s32[512]{0:T(512)} %param.3) | copy-start | bytes 6148
  10.1 81.4 %all-to-all-start = ((f32[8,3,192,128]{2,0,1,3:T(8,128)}), f32[8,3,192,128]{2,0,1,3:T(8,128)S(1)}, u32[]{:S(2)}, u32[]{:S(2)}) async-start(f32[8,3,192,128]{2,0,1,3:T(8,128)} %copy.26), calls=%async_computation | async-start | bytes 6291456 | tf_op jit(solution)/shard_map/all_to_all | solution.py:62
  20.5 120.0 %reduce-scatter.2.cloned.1.call-start = ((), (), s32[]{:S(2)}) async-start(), calls=%async_computation.3 | async-start | bytes 2654208 | tf_op jit(solution)/shard_map/reduce_scatter | solution.py:37
  91.5 50.8 %copy-start.1 = (f32[8,3,192,128]{2,0,1,3:T(8,128)}, f32[8,3,192,128]{2,0,1,3:T(8,128)S(1)}, u32[]{:S(2)}) copy-start(f32[8,3,192,128]{2,0,1,3:T(8,128)S(1)} %all-to-all-done) | copy-start | bytes 7077892
  91.5 1.2 copy-start.2
  98.0 88.7 %all-gather.2.cloned.1.call-start = ((), (), s32[]{:S(2)}) async-start(), calls=%async_computation.4 | async-start | bytes 2654208 | tf_op jit(solution)/shard_map/all_gather | solution.py:46
  142.3 46.5 %copy-start.3 = (f32[192,384]{1,0:T(8,128)S(1)}, f32[192,384]{1,0:T(8,128)}, u32[]{:S(2)}) copy-start(f32[192,384]{1,0:T(8,128)} %get-tuple-element.10) | copy-start | bytes 884740
  190.8 1.7 slice-start
Sparse Core Ops, SparseCore 0:
  98.1 42.3 reduce-scatter.1
  142.6 44.1 all-gather.1
where the time goes:
time: 286 us
  waiting for transfers between devices  155 us (54%)
  blocking collectives  84.5 us (30%)
  between operations  13.6 us (5%)
  local copies, waits for them, and re-layouts  10.6 us (4%)
  starting transfers between devices  10.4 us (4%)
  matrix products  7.4 us (3%)
  other arithmetic  4.12 us (1%)
    all_to_all x1, blocking collectives, on_device(): lax.all_to_all(rebuilt, 'theta', split_axis=3, concat_axis=3, tiled=True)  84.5 us
    all_to_all x1, waiting for transfers between devices, on_device(): lax.all_to_all(fields, 'theta', split_axis=3, concat_axis=3, tiled=True)  68.9 us
    all_gather x1, waiting for transfers between devices, spectral(): piece = lax.all_gather(masked, 'phi', axis=0, tiled=True)  44.4 us
    reduce_scatter x1, waiting for transfers between devices, spectral(): lax.psum_scatter(out.reshape(share_rows * lax.axis_size('phi'), groups *...  42.2 us
    all_to_all x1, starting transfers between devices, on_device(): lax.all_to_all(fields, 'theta', split_axis=3, concat_axis=3, tiled=True)  10.4 us
  transfers between devices with their start and end apart: 3, of which 3 were waited for; matrix products, arithmetic and copies ran while one was open for 1% of the time, Pallas kernels for 0%

commit v1 on v0

v1 whole, which is shorter than its diff:
```python
import math

import jax
import jax.numpy as jnp
import numpy as np
from jax import lax
from jax.experimental import pallas as pl
from jax.experimental.pallas import tpu as pltpu
from jax.sharding import PartitionSpec as P

KMAX = 384
NPHI = 1536
SEG = 8
LOC = NPHI // SEG
MODES = KMAX // SEG


def class_modes():
    m = SEG * np.arange(MODES)
    return [m, m + 4], [(m + p, m + SEG - p) for p in (1, 2, 3)]


def cos_sin(k):
    turns = (k[:, None] * np.arange(LOC)[None, :]) % NPHI
    angle = turns * (2.0 * math.pi / NPHI)
    return np.cos(angle), np.sin(angle)


def split(table):
    high = table.astype(jnp.bfloat16)
    low = (table - high.astype(np.float64)).astype(jnp.bfloat16)
    return high, low


def tables():
    real, paired = class_modes()
    mr = np.stack([np.concatenate(cos_sin(k)) for k in real])
    rows = []
    for kp, kn in paired:
        cp, sp = cos_sin(kp)
        cn, sn = cos_sin(kn)
        rows.append(
            np.concatenate(
                [
                    np.concatenate([cp, -sp], 1),
                    np.concatenate([cn, sn], 1),
                    np.concatenate([sp, cp], 1),
                    np.concatenate([sn, -cn], 1),
                ]
            )
        )
    mp = np.stack(rows)
    kr = np.stack([np.concatenate([k, k]) for k in real])
    kp = np.stack([np.concatenate([a, b, a, b]) for a, b in paired])
    modes = np.concatenate([kr.reshape(-1), kp.reshape(-1)]).astype(np.int32)
    return mr, mp, modes


def dot(a, b):
    return lax.dot_general(a, b, (((1,), (0,)), ((), ())), preferred_element_type=jnp.float32)


def dot3(high, low, x):
    xh = x.astype(jnp.bfloat16)
    xl = (x - xh.astype(jnp.float32)).astype(jnp.bfloat16)
    return dot(high, xh) + (dot(high, xl) + dot(low, xh))


HALF = math.sqrt(0.5)


def filter_body(y_ref, counts_ref, modes_ref, arh, arl, aph, apl, brh, brl, bph, bpl, o_ref):
    counts = counts_ref[...]
    f = [y_ref[s] for s in range(SEG)]
    e = [f[i] + f[i + 4] for i in range(4)]
    o = [f[i] - f[i + 4] for i in range(4)]
    e02, e13 = e[0] + e[2], e[1] + e[3]
    od, os_ = HALF * (o[1] - o[3]), HALF * (o[1] + o[3])
    real = [e02 + e13, e02 - e13]
    pair = [
        (o[0] + od, o[2] + os_),
        (e[0] - e[2], e[1] - e[3]),
        (o[0] - od, os_ - o[2]),
    ]

    def keep(coef, at):
        k = modes_ref[at : at + coef.shape[0], :]
        weight = jnp.where(k == 0, 1.0 / NPHI, 2.0 / NPHI)
        return jnp.where(k < counts, coef * weight, 0.0)

    u = []
    for i in range(2):
        coef = keep(dot3(arh[i], arl[i], real[i]), i * 2 * MODES)
        u.append(dot3(brh[i], brl[i], coef))
    uv = []
    for i in range(3):
        x = jnp.concatenate(pair[i], axis=0)
        coef = keep(dot3(aph[i], apl[i], x), 4 * MODES + i * 4 * MODES)
        r = dot3(bph[i], bpl[i], coef)
        uv.append((r[:LOC], r[LOC:]))
    (u1, v1), (u2, v2), (u3, v3) = uv
    su, du = u[0] + u[1], u[0] - u[1]
    p = [su + u2, du + v2, su - u2, du - v2]
    d13, s13 = HALF * (u1 - u3), HALF * (v1 + v3)
    q = [u1 + u3, s13 + d13, v1 - v3, s13 - d13]
    for s in range(4):
        o_ref[s] = p[s] + q[s]
        o_ref[s + 4] = p[s] - q[s]


def solution(mesh):
    n_theta = mesh.shape["theta"]
    mr, mp, modes = tables()
    consts = (
        *split(mr),
        *split(mp),
        *split(np.swapaxes(mr, 1, 2)),
        *split(np.swapaxes(mp, 1, 2)),
    )
    modes = np.ascontiguousarray(np.broadcast_to(modes[:, None], (modes.size, 128)))
    last = n_theta - 1
    outward = [(0, 2), (1, 3), (last - 1, last - 3), (last, last - 2)]
    inward = [(b, a) for a, b in outward]

    def exchange(v):
        return lax.all_to_all(v, "phi", split_axis=0, concat_axis=0, tiled=True)

    def filter_lines(lines, counts):
        return pl.pallas_call(
            filter_body,
            out_shape=jax.ShapeDtypeStruct(lines.shape, jnp.float32),
            name="filter_lines",
        )(lines, counts, jnp.asarray(modes), *[jnp.asarray(c) for c in consts])

    def on_device(fields, kept_counts):
        theta = lax.axis_index("theta")
        is_cap = (theta < 2) | (theta > last - 2)
        is_helper = ((theta >= 2) & (theta < 4)) | ((theta > last - 4) & (theta <= last - 2))
        band = theta % 2 + jnp.where(theta < n_theta // 2, 0, 2)
        rows = fields.shape[3]
        counts = lax.dynamic_slice(kept_counts, (band * rows,), (rows,)).reshape(1, rows)
        x0, x1, x2 = fields[:, 0], fields[:, 1], fields[:, 2]
        moved = lax.ppermute(x2, "theta", outward)
        lines0 = exchange(x0)
        lines1 = exchange(jnp.where(is_helper, moved, x1))
        done0 = filter_lines(lines0, counts)
        done1 = filter_lines(lines1, counts)
        back0 = exchange(jnp.where(is_helper, done1, done0))
        back1 = exchange(done1)
        back2 = lax.ppermute(back0, "theta", inward)
        out = jnp.stack([back0, back1, back2], axis=1)
        return jnp.where(is_cap, out, fields)

    return jax.shard_map(
        on_device,
        mesh=mesh,
        in_specs=(P(None, "row", "phi", "theta"), P()),
        out_specs=P(None, "row", "phi", "theta"),
        check_vma=False,
    )
```

time: 286 us -> 127 us (0.44)
  waiting for transfers between devices: 155 us -> 58.8 us
  blocking collectives: 84.5 us -> 25.5 us
  starting transfers between devices: 10.4 us -> 24.7 us
  between operations: 13.6 us -> 0.07 us
  Pallas kernels: 0 us -> 9.57 us
  matrix products: 7.4 us -> 0 us
  local copies, waits for them, and re-layouts: 10.6 us -> 4.99 us
    all_to_all x1, blocking collectives: 84.5 us -> 25.5 us  [exchange(): return lax.all_to_all(v, 'phi', split_axis=0, concat_axis=0, tiled=True)]
    all_gather x1 -> x0, waiting for transfers between devices: 44.4 us -> none  [spectral(): piece = lax.all_gather(masked, 'phi', axis=0, tiled=True)]
    reduce_scatter x1 -> x0, waiting for transfers between devices: 42.2 us -> none  [spectral(): lax.psum_scatter(out.reshape(share_rows * lax.axis_size('phi'), groups *...]
    all_to_all x1 -> x3, waiting for transfers between devices: 68.9 us -> 43.5 us  [exchange(): return lax.all_to_all(v, 'phi', split_axis=0, concat_axis=0, tiled=True)]
    ppermute x0 -> x2, waiting for transfers between devices: none -> 15.3 us  [the longest x1 15.3 us: on_device(): moved = lax.ppermute(x2, 'theta', outward)]
    pallas_call x0 -> x2, Pallas kernels: none -> 9.57 us  [filter_lines(): pl.pallas_call(filter_body, out_shape=jax.ShapeDtypeStruct(lines.shape, j...]
    all_to_all x1 -> x3, starting transfers between devices: 10.4 us -> 19.3 us  [exchange(): return lax.all_to_all(v, 'phi', split_axis=0, concat_axis=0, tiled=True)]
    dot_general x2 -> x0, matrix products: 7.4 us -> none  [the longest x1 5.38 us: spectral(): jnp.einsum('pk,gpr->kgr', forward, grouped, precision=highest, preferred_...]
  transfers between devices with their start and end apart: 3 -> 5, of which waited for: 3 -> 4; matrix products, arithmetic and copies ran while one was open for 1% -> 1% of each run, Pallas kernels for 0% -> 4%
where the time goes in v1:
time: 127 us
  waiting for transfers between devices  58.8 us (46%)
  blocking collectives  25.5 us (20%)
  starting transfers between devices  24.7 us (19%)
  Pallas kernels  9.57 us (8%)
  local copies, waits for them, and re-layouts  4.99 us (4%)
  other arithmetic  2.94 us (2%)
    all_to_all x3, waiting for transfers between devices, exchange(): return lax.all_to_all(v, 'phi', split_axis=0, concat_axis=0, tiled=True)  43.5 us
    all_to_all x1, blocking collectives, exchange(): return lax.all_to_all(v, 'phi', split_axis=0, concat_axis=0, tiled=True)  25.5 us
    all_to_all x3, starting transfers between devices, exchange(): return lax.all_to_all(v, 'phi', split_axis=0, concat_axis=0, tiled=True)  19.3 us
    ppermute x1, waiting for transfers between devices, on_device(): moved = lax.ppermute(x2, 'theta', outward)  15.3 us
    pallas_call x2, Pallas kernels, filter_lines(): pl.pallas_call(filter_body, out_shape=jax.ShapeDtypeStruct(lines.shape, j...  9.57 us
    ppermute x1, starting transfers between devices, on_device(): moved = lax.ppermute(x2, 'theta', outward)  4.1 us
    squeeze x1, local copies, waits for them, and re-layouts, on_device(): x0, x1, x2 = (fields[:, 0], fields[:, 1], fields[:, 2])  2.82 us
  transfers between devices with their start and end apart: 5, of which 4 were waited for; matrix products, arithmetic and copies ran while one was open for 1% of the time, Pallas kernels for 4%

profile of v1, /device:TPU:1, one launch (start us, length us, event | category | flops | bytes accessed | tf_op | source)
XLA Modules:
  0.0 126.6 jit_solution(1603702839225346921)
XLA Ops:
  0.0 0.0 copy-start
  0.0 0.0 copy-start.1
  0.0 2.8 %slice_bitcast_fusion = (f32[8,192,128]{2,1,0:T(8,128)}, f32[8,192,128]{2,1,0:T(8,128)}) fusion(f32[8,3,192,128]{3,2,1,0:T(8,128)} %param.11), kind=kLoop, calls=%fused_computation.1 | loop fusion | bytes 3145728 | tf_op jit(solution)/shard_map/squeeze | solution.py:142
  2.8 10.9 %all-to-all-start.1 = ((f32[8,192,128]{2,1,0:T(8,128)}), f32[8,192,128]{2,1,0:T(8,128)S(1)}, u32[]{:S(2)}, u32[]{:S(2)}) async-start(f32[8,192,128]{2,1,0:T(8,128)} %get-tuple-element.5), calls=%async_computation.1 | async-start | bytes 1572864 | tf_op jit(solution)/shard_map/all_to_all | solution.py:126
  13.7 4.1 %collective-permute-start = (f32[8,192,128]{2,1,0:T(8,128)}, f32[8,192,128]{2,1,0:T(8,128)}, u32[]{:S(2)}, u32[]{:S(2)}) collective-permute-start(f32[8,192,128]{2,1,0:T(8,128)} %get-tuple-element.6), channel_id=1, source_target_pairs={{0,8},{4,12},{56,48},{60,52},{1,9},{5,13},{57,49},{61,53},{2,10},{... | collective-permute-start | bytes 2359304 | tf_op jit(solution)/shard_map/ppermute | solution.py:143
  17.8 15.3 %collective-permute-done = f32[8,192,128]{2,1,0:T(8,128)} collective-permute-done((f32[8,192,128]{2,1,0:T(8,128)}, f32[8,192,128]{2,1,0:T(8,128)}, u32[]{:S(2)}, u32[]{:S(2)}) %collective-permute-start) | collective-permute-done | bytes 786464 | tf_op jit(solution)/shard_map/ppermute | solution.py:143
  33.1 0.0 copy-done.1
  33.1 1.0 fusion
  34.2 3.1 %all-to-all-done.1.y_ref = f32[8,192,128]{2,1,0:T(8,128)S(1)} async-done(((f32[8,192,128]{2,1,0:T(8,128)}), f32[8,192,128]{2,1,0:T(8,128)S(1)}, u32[]{:S(2)}, u32[]{:S(2)}) %all-to-all-start.1) | async-done | bytes 786464 | tf_op jit(solution)/shard_map/all_to_all | solution.py:126
  37.3 0.0 copy-start.3
  37.3 4.2 %all-to-all-start = ((f32[8,192,128]{2,1,0:T(8,128)}), f32[8,192,128]{2,1,0:T(8,128)}, u32[]{:S(2)}, u32[]{:S(2)}) async-start(f32[8,192,128]{2,1,0:T(8,128)} %fusion), calls=%async_computation | async-start | bytes 1572864 | tf_op jit(solution)/shard_map/all_to_all | solution.py:126
  41.5 0.0 copy-done
  41.5 0.6 dynamic-slice_bitcast_fusion.counts_ref
  42.1 0.0 copy-done.3
  42.1 4.8 %filter_lines.3 = f32[8,192,128]{2,1,0:T(8,128)} custom-call(f32[8,192,128]{2,1,0:T(8,128)} %copy-done.3, s32[1,128]{1,0:T(1,128)} %dynamic-slice_bitcast_fusion.counts_ref, s32[768,128]{1,0:T(8,128)} %constant.50.clone.modes_ref, bf16[2,96,192]{2,1,0:T(8,128)(2,1)} %constant.51.clone.arh, bf16[2,96,192]{2,1,0:T(8,128)(2,1)} %constant.52.clone.arl, ...), custom_call_target="tpu_custom_call" | custom-call | tf_op jit(solution)/shard_map/filter_lines/pallas_call | solution.py:129
  46.9 0.0 copy-start.2
  46.9 18.1 %all-to-all-done.y_ref = f32[8,192,128]{2,1,0:T(8,128)} async-done(((f32[8,192,128]{2,1,0:T(8,128)}), f32[8,192,128]{2,1,0:T(8,128)}, u32[]{:S(2)}, u32[]{:S(2)}) %all-to-all-start) | async-done | bytes 786464 | tf_op jit(solution)/shard_map/all_to_all | solution.py:126
  65.0 4.8 %filter_lines.2 = f32[8,192,128]{2,1,0:T(8,128)} custom-call(f32[8,192,128]{2,1,0:T(8,128)} %all-to-all-done.y_ref, s32[1,128]{1,0:T(1,128)} %dynamic-slice_bitcast_fusion.counts_ref, s32[768,128]{1,0:T(8,128)} %constant.50.clone.modes_ref, bf16[2,96,192]{2,1,0:T(8,128)(2,1)} %constant.51.clone.arh, bf16[2,96,192]{2,1,0:T(8,128)(2,1)} %constant.52.clone.arl, ...), custom_call_target="tpu_custom_call" | custom-call | tf_op jit(solution)/shard_map/filter_lines/pallas_call | solution.py:129
  69.8 0.0 copy-done.2
  69.8 0.1 broadcast_select_fusion
  70.0 25.5 %all_to_all.20 = f32[8,192,128]{2,1,0:T(8,128)S(1)} all-to-all(f32[8,192,128]{2,1,0:T(8,128)S(1)} %broadcast_select_fusion), channel_id=1, replica_groups=mesh['phi'=8,'theta'=16,'row'=4] {'phi'}, dimensions={0} | all-to-all | bytes 1572864 | tf_op jit(solution)/shard_map/all_to_all | solution.py:126
  95.5 4.2 %all-to-all-start.3 = ((f32[8,192,128]{2,1,0:T(8,128)}), f32[8,192,128]{2,1,0:T(8,128)}, u32[]{:S(2)}, u32[]{:S(2)}) async-start(f32[8,192,128]{2,1,0:T(8,128)} %filter_lines.2), calls=%async_computation.3 | async-start | bytes 1572864 | tf_op jit(solution)/shard_map/all_to_all | solution.py:126
  99.7 1.3 %collective-permute-start.1 = (f32[8,192,128]{2,1,0:T(8,128)S(1)}, f32[8,192,128]{2,1,0:T(8,128)}, u32[]{:S(2)}, u32[]{:S(2)}) collective-permute-start(f32[8,192,128]{2,1,0:T(8,128)S(1)} %all_to_all.20), channel_id=1, source_target_pairs={{8,0},{12,4},{48,56},{52,60},{9,1},{13,5},{49,57},{53,61},{10,2},{... | collective-permute-start | bytes 2359304 | tf_op jit(solution)/shard_map/ppermute | solution.py:150
  101.0 22.3 %all-to-all-done.3 = f32[8,192,128]{2,1,0:T(8,128)} async-done(((f32[8,192,128]{2,1,0:T(8,128)}), f32[8,192,128]{2,1,0:T(8,128)}, u32[]{:S(2)}, u32[]{:S(2)}) %all-to-all-start.3) | async-done | bytes 786464 | tf_op jit(solution)/shard_map/all_to_all | solution.py:126
  123.2 0.0 collective-permute-done.1
  123.2 1.8 %maximum_select_fusion = f32[8,3,192,128]{3,2,0,1:T(8,128)S(1)} fusion(f32[8,1,192,128]{3,2,0,1:T(8,128)} %bitcast.6, f32[8,1,192,128]{3,2,0,1:T(8,128)} %bitcast.5, f32[8,1,192,128]{3,2,0,1:T(8,128)S(1)} %bitcast.13, pred[]{:T(512)S(6)} %or.6, f32[8,3,192,128]{3,2,1,0:T(8,128)S(1)} %copy-done.1), kind=kLoop, calls=%fused_computation | loop fusion | flops 1769472 | bytes 7077889 | tf_op jit(solution)/shard_map/jit(_where)/select_n | solution.py:152
  125.0 1.6 %copy.16 = f32[8,3,192,128]{3,2,1,0:T(8,128)} copy(f32[8,3,192,128]{3,2,0,1:T(8,128)S(1)} %maximum_select_fusion) | data formatting | bytes 4718592 | tf_op jit(solution)/shard_map/jit(_where)/select_n | solution.py:152
Async XLA Ops:
  0.0 41.5 %copy-start = (s32[512]{0:T(512)S(1)}, s32[512]{0:T(512)}, u32[]{:S(2)}) copy-start(s32[512]{0:T(512)} %param.12) | copy-start | bytes 6148
  0.0 33.1 %copy-start.1 = (f32[8,3,192,128]{3,2,1,0:T(8,128)S(1)}, f32[8,3,192,128]{3,2,1,0:T(8,128)}, u32[]{:S(2)}) copy-start(f32[8,3,192,128]{3,2,1,0:T(8,128)} %param.11) | copy-start | bytes 7077892
  2.8 34.4 %all-to-all-start.1 = ((f32[8,192,128]{2,1,0:T(8,128)}), f32[8,192,128]{2,1,0:T(8,128)S(1)}, u32[]{:S(2)}, u32[]{:S(2)}) async-start(f32[8,192,128]{2,1,0:T(8,128)} %get-tuple-element.5), calls=%async_computation.1 | async-start | bytes 1572864 | tf_op jit(solution)/shard_map/all_to_all | solution.py:126
  13.7 19.4 %collective-permute-start = (f32[8,192,128]{2,1,0:T(8,128)}, f32[8,192,128]{2,1,0:T(8,128)}, u32[]{:S(2)}, u32[]{:S(2)}) collective-permute-start(f32[8,192,128]{2,1,0:T(8,128)} %get-tuple-element.6), channel_id=1, source_target_pairs={{0,8},{4,12},{56,48},{60,52},{1,9},{5,13},{57,49},{61,53},{2,10},{... | collective-permute-start | bytes 2359304 | tf_op jit(solution)/shard_map/ppermute | solution.py:143
  37.3 4.8 %copy-start.3 = (f32[8,192,128]{2,1,0:T(8,128)}, f32[8,192,128]{2,1,0:T(8,128)S(1)}, u32[]{:S(2)}) copy-start(f32[8,192,128]{2,1,0:T(8,128)S(1)} %all-to-all-done.1.y_ref) | copy-start | bytes 2359300
  37.3 27.8 %all-to-all-start = ((f32[8,192,128]{2,1,0:T(8,128)}), f32[8,192,128]{2,1,0:T(8,128)}, u32[]{:S(2)}, u32[]{:S(2)}) async-start(f32[8,192,128]{2,1,0:T(8,128)} %fusion), calls=%async_computation | async-start | bytes 1572864 | tf_op jit(solution)/shard_map/all_to_all | solution.py:126
  46.9 22.9 %copy-start.2 = (f32[8,192,128]{2,1,0:T(8,128)S(1)}, f32[8,192,128]{2,1,0:T(8,128)}, u32[]{:S(2)}) copy-start(f32[8,192,128]{2,1,0:T(8,128)} %filter_lines.3) | copy-start | bytes 2359300
  95.5 27.8 %all-to-all-start.3 = ((f32[8,192,128]{2,1,0:T(8,128)}), f32[8,192,128]{2,1,0:T(8,128)}, u32[]{:S(2)}, u32[]{:S(2)}) async-start(f32[8,192,128]{2,1,0:T(8,128)} %filter_lines.2), calls=%async_computation.3 | async-start | bytes 1572864 | tf_op jit(solution)/shard_map/all_to_all | solution.py:126
  99.7 23.6 %collective-permute-start.1 = (f32[8,192,128]{2,1,0:T(8,128)S(1)}, f32[8,192,128]{2,1,0:T(8,128)}, u32[]{:S(2)}, u32[]{:S(2)}) collective-permute-start(f32[8,192,128]{2,1,0:T(8,128)S(1)} %all_to_all.20), channel_id=1, source_target_pairs={{8,0},{12,4},{48,56},{52,60},{9,1},{13,5},{49,57},{53,61},{10,2},{... | collective-permute-start | bytes 2359304 | tf_op jit(solution)/shard_map/ppermute | solution.py:150

commit v2 on v1

v2 whole, which is shorter than its diff:
```python
import math

import jax
import jax.numpy as jnp
import numpy as np
from jax import lax
from jax.experimental import pallas as pl
from jax.experimental.pallas import tpu as pltpu
from jax.sharding import PartitionSpec as P

KMAX = 384
NPHI = 1536
SEG = 8
LOC = NPHI // SEG
MODES = KMAX // SEG


def class_modes():
    m = SEG * np.arange(MODES)
    return [m, m + 4], [(m + p, m + SEG - p) for p in (1, 2, 3)]


def cos_sin(k):
    turns = (k[:, None] * np.arange(LOC)[None, :]) % NPHI
    angle = turns * (2.0 * math.pi / NPHI)
    return np.cos(angle), np.sin(angle)


def split(table):
    high = table.astype(jnp.bfloat16)
    low = (table - high.astype(np.float64)).astype(jnp.bfloat16)
    return np.concatenate([high, low], axis=-2)


def tables():
    real, paired = class_modes()
    mr = np.stack([np.concatenate(cos_sin(k)) for k in real])
    rows = []
    for kp, kn in paired:
        cp, sp = cos_sin(kp)
        cn, sn = cos_sin(kn)
        rows.append(
            np.concatenate(
                [
                    np.concatenate([cp, -sp], 1),
                    np.concatenate([cn, sn], 1),
                    np.concatenate([sp, cp], 1),
                    np.concatenate([sn, -cn], 1),
                ]
            )
        )
    mp = np.stack(rows)
    kr = np.stack([np.concatenate([k, k]) for k in real])
    kp = np.stack([np.concatenate([a, b, a, b]) for a, b in paired])
    modes = np.concatenate([kr.reshape(-1), kp.reshape(-1)]).astype(np.int32)
    return mr, mp, modes


def dot(parts, x):
    high = x.astype(jnp.bfloat16)
    low = (x - high.astype(jnp.float32)).astype(jnp.bfloat16)
    both = jnp.concatenate([high, low], axis=1)
    r = lax.dot_general(parts, both, (((1,), (0,)), ((), ())), preferred_element_type=jnp.float32)
    n, c = parts.shape[0] // 2, x.shape[1]
    return r[:n, :c] + (r[:n, c:] + r[n:, :c] + r[n:, c:])


HALF = math.sqrt(0.5)


def filter_lines(y, counts, modes, ar, ap, br, bp):
    e = [y[i] + y[i + 4] for i in range(4)]
    o = [y[i] - y[i + 4] for i in range(4)]
    e02, e13 = e[0] + e[2], e[1] + e[3]
    od, os_ = HALF * (o[1] - o[3]), HALF * (o[1] + o[3])
    real = [e02 + e13, e02 - e13]
    pair = [
        (o[0] + od, o[2] + os_),
        (e[0] - e[2], e[1] - e[3]),
        (o[0] - od, os_ - o[2]),
    ]

    def keep(coef, at):
        k = modes[at : at + coef.shape[0], :]
        weight = jnp.where(k == 0, 1.0 / NPHI, 2.0 / NPHI)
        return jnp.where(k < counts, coef * weight, 0.0)

    u = [dot(br[i], keep(dot(ar[i], real[i]), i * 2 * MODES)) for i in range(2)]
    uv = []
    for i in range(3):
        coef = dot(ap[i], jnp.concatenate(pair[i], axis=0))
        r = dot(bp[i], keep(coef, 4 * MODES + i * 4 * MODES))
        uv.append((r[:LOC], r[LOC:]))
    (u1, v1), (u2, v2), (u3, v3) = uv
    su, du = u[0] + u[1], u[0] - u[1]
    p = [su + u2, du + v2, su - u2, du - v2]
    d13, s13 = HALF * (u1 - u3), HALF * (v1 + v3)
    q = [u1 + u3, s13 + d13, v1 - v3, s13 - d13]
    return [p[i] + q[i] for i in range(4)] + [p[i] - q[i] for i in range(4)]


def filter_kernel(cap_ref, y_ref, counts_ref, modes_ref, ar, ap, br, bp, o_ref):
    is_cap = cap_ref[0] > 0
    shells = y_ref.shape[1]

    @pl.when(is_cap)
    def _():
        @pl.loop(0, shells)
        def _(i):
            y = [y_ref[s, i] for s in range(SEG)]
            done = filter_lines(y, counts_ref[...], modes_ref, ar, ap, br, bp)
            for s in range(SEG):
                o_ref[s, i] = done[s]

    @pl.when(jnp.logical_not(is_cap))
    def _():
        o_ref[...] = y_ref[...]


def solution(mesh):
    last = mesh.shape["theta"] - 1
    mr, mp, modes = tables()
    modes = np.ascontiguousarray(np.broadcast_to(modes[:, None], (modes.size, 128)))
    consts = (modes, split(mr), split(mp), split(np.swapaxes(mr, 1, 2)), split(np.swapaxes(mp, 1, 2)))

    def exchange(v):
        return lax.all_to_all(v, "phi", split_axis=0, concat_axis=0, tiled=True)

    def filtered(lines, counts, is_cap):
        vmem = pl.BlockSpec(memory_space=pltpu.VMEM)
        return pl.pallas_call(
            filter_kernel,
            out_shape=jax.ShapeDtypeStruct(lines.shape, jnp.float32),
            in_specs=[pl.BlockSpec(memory_space=pltpu.SMEM)] + [vmem] * 7,
            out_specs=vmem,
            compiler_params=pltpu.CompilerParams(vmem_limit_bytes=16 << 20),
            name="filter_lines",
        )(is_cap.astype(jnp.int32).reshape(1), lines, counts, *[jnp.asarray(c) for c in consts])

    def on_device(fields, kept_counts):
        theta = lax.axis_index("theta")
        is_cap = (theta < 2) | (theta > last - 2)
        band = jnp.where(theta < 2, theta, theta - (last - 3)) % 4
        rows = fields.shape[3]
        counts = lax.dynamic_slice(kept_counts, (band * rows,), (rows,)).reshape(1, rows)
        return exchange(filtered(exchange(fields), counts, is_cap))

    return jax.shard_map(
        on_device,
        mesh=mesh,
        in_specs=(P(None, "row", "phi", "theta"), P()),
        out_specs=P(None, "row", "phi", "theta"),
        check_vma=False,
    )
```

time: 127 us -> 138 us (1.087)
  blocking collectives: 25.5 us -> 59.6 us
  starting transfers between devices: 24.7 us -> 11 us
  Pallas kernels: 9.57 us -> 4.28 us
  other arithmetic: 2.94 us -> 0 us
  waiting for transfers between devices: 58.8 us -> 57.2 us
    all_to_all x1, blocking collectives: 25.5 us -> 59.6 us  [exchange(): return lax.all_to_all(v, 'phi', split_axis=0, concat_axis=0, tiled=True)]
    ppermute x2 -> x0, waiting for transfers between devices: 15.3 us -> none  [the longest x1 15.3 us: on_device(): moved = lax.ppermute(x2, 'theta', outward)]
    all_to_all x3 -> x1, waiting for transfers between devices: 43.5 us -> 57.2 us  [exchange(): return lax.all_to_all(v, 'phi', split_axis=0, concat_axis=0, tiled=True)]
    all_to_all x3 -> x1, starting transfers between devices: 19.3 us -> 11 us  [exchange(): return lax.all_to_all(v, 'phi', split_axis=0, concat_axis=0, tiled=True)]
    unnamed x8 -> x13, local copies, waits for them, and re-layouts: 0.02 us -> 5.43 us
    ppermute x2 -> x0, starting transfers between devices: 5.39 us -> none  [the longest x1 4.1 us: on_device(): moved = lax.ppermute(x2, 'theta', outward)]
    pallas_call x2 -> x1, Pallas kernels: 9.57 us -> 4.28 us  [filtered(): pl.pallas_call(filter_kernel, out_shape=jax.ShapeDtypeStruct(lines.shape,...]
    select_n x3 -> x0, other arithmetic: 2.94 us -> none  [the longest x1 1.77 us: on_device(): return jnp.where(is_cap, out, fields)]
  transfers between devices with their start and end apart: 5 -> 1, of which waited for: 4 -> 1; matrix products, arithmetic and copies ran while one was open for 1% -> 0% of each run, Pallas kernels for 4% -> 0%
where the time goes in v2:
time: 138 us
  blocking collectives  59.6 us (43%)
  waiting for transfers between devices  57.2 us (41%)
  starting transfers between devices  11 us (8%)
  local copies, waits for them, and re-layouts  5.51 us (4%)
  Pallas kernels  4.28 us (3%)
    all_to_all x1, blocking collectives, exchange(): return lax.all_to_all(v, 'phi', split_axis=0, concat_axis=0, tiled=True)  59.6 us
    all_to_all x1, waiting for transfers between devices, exchange(): return lax.all_to_all(v, 'phi', split_axis=0, concat_axis=0, tiled=True)  57.2 us
    all_to_all x1, starting transfers between devices, exchange(): return lax.all_to_all(v, 'phi', split_axis=0, concat_axis=0, tiled=True)  11 us
    unnamed x13, local copies, waits for them, and re-layouts  5.43 us
    pallas_call x1, Pallas kernels, filtered(): pl.pallas_call(filter_kernel, out_shape=jax.ShapeDtypeStruct(lines.shape,...  4.28 us
  transfers between devices with their start and end apart: 1, of which 1 were waited for; matrix products, arithmetic and copies ran while one was open for 0% of the time, Pallas kernels for 0%

profile of v2, /device:TPU:1, one launch (start us, length us, event | category | flops | bytes accessed | tf_op | source)
XLA Modules:
  0.0 137.6 jit_solution(13091369090861071738)
XLA Ops:
  0.0 0.0 copy-start
  0.0 0.0 copy-start.1
  0.0 11.0 %all-to-all-start = ((f32[8,3,192,128]{3,2,1,0:T(8,128)}), f32[8,3,192,128]{3,2,1,0:T(8,128)S(1)}, u32[]{:S(2)}, u32[]{:S(2)}) async-start(f32[8,3,192,128]{3,2,1,0:T(8,128)} %param.7), calls=%async_computation | async-start | bytes 4718592 | tf_op jit(solution)/shard_map/all_to_all | solution.py:127
  11.0 0.0 copy-done
  11.0 0.1 dynamic-slice_bitcast_fusion.counts_ref
  11.1 57.2 %all-to-all-done.y_ref = f32[8,3,192,128]{3,2,1,0:T(8,128)S(1)} async-done(((f32[8,3,192,128]{3,2,1,0:T(8,128)}), f32[8,3,192,128]{3,2,1,0:T(8,128)S(1)}, u32[]{:S(2)}, u32[]{:S(2)}) %all-to-all-start) | async-done | bytes 2359328 | tf_op jit(solution)/shard_map/all_to_all | solution.py:127
  68.3 0.0 copy-done.1
  68.3 0.0 copy-start.2
  68.3 1.2 copy-done.2
  69.5 0.0 copy-start.3
  69.5 1.0 copy-done.3
  70.5 0.0 copy-start.4
  70.5 0.9 copy-done.4
  71.4 0.0 copy-start.5
  71.4 0.9 copy-done.5
  72.3 4.3 %filter_lines.1 = f32[8,3,192,128]{3,2,1,0:T(8,128)S(1)} custom-call(s32[1]{0:T(128)} %bitcast.cap_ref, f32[8,3,192,128]{3,2,1,0:T(8,128)S(1)} %all-to-all-done.y_ref, s32[1,128]{1,0:T(1,128)S(1)} %dynamic-slice_bitcast_fusion.counts_ref, s32[768,128]{1,0:T(8,128)S(1)} %copy-done.3, bf16[2,192,192]{2,1,0:T(8,128)(2,1)S(1)} %copy-done.5, ...), custom_call_target="tpu_custom_call" | custom-call | tf_op jit(solution)/shard_map/filter_lines/pallas_call | solution.py:131
  76.6 59.6 %all_to_all.10 = f32[8,3,192,128]{3,2,1,0:T(8,128)S(1)} all-to-all(f32[8,3,192,128]{3,2,1,0:T(8,128)S(1)} %filter_lines.1), channel_id=1, replica_groups=mesh['phi'=8,'theta'=16,'row'=4] {'phi'}, dimensions={0} | all-to-all | bytes 4718592 | tf_op jit(solution)/shard_map/all_to_all | solution.py:127
  136.2 1.4 %copy.9 = f32[8,3,192,128]{3,2,1,0:T(8,128)} copy(f32[8,3,192,128]{3,2,1,0:T(8,128)S(1)} %all_to_all.10) | data formatting | bytes 4718592
Async XLA Ops:
  0.0 11.0 %copy-start = (s32[512]{0:T(512)S(1)}, s32[512]{0:T(512)}, u32[]{:S(2)}) copy-start(s32[512]{0:T(512)} %param.8) | copy-start | bytes 6148
  0.0 68.3 %copy-start.1 = (bf16[3,768,192]{2,1,0:T(8,128)(2,1)S(1)}, bf16[3,768,192]{2,1,0:T(8,128)(2,1)}, u32[]{:S(2)}) copy-start(bf16[3,768,192]{2,1,0:T(8,128)(2,1)} %constant.45.clone.bp) | copy-start | bytes 2654212
  0.0 68.3 %all-to-all-start = ((f32[8,3,192,128]{3,2,1,0:T(8,128)}), f32[8,3,192,128]{3,2,1,0:T(8,128)S(1)}, u32[]{:S(2)}, u32[]{:S(2)}) async-start(f32[8,3,192,128]{3,2,1,0:T(8,128)} %param.7), calls=%async_computation | async-start | bytes 4718592 | tf_op jit(solution)/shard_map/all_to_all | solution.py:127
  68.3 1.2 copy-start.2
  69.5 1.0 copy-start.3
  70.5 0.9 copy-start.4
  71.4 0.9 copy-start.5
